TPU v7x, 32 devices: a whole 2x2x4 slice. The times are simulated.
32 devices in a mesh: grp: 8 (over z, core), sp: 4 (over y, x).
Axes of the slice: x: 2, y: 2, z: 4, core: 2. Of those that a mesh axis runs over, the one named last changes fastest.
Arguments:
- acts: bfloat16 [32, 4, 16, 728], P('grp', 'sp'), may hold values from -6 to 6
- cotangent: bfloat16 [32, 4, 16, 728], P(('grp', 'sp')), may hold values from -6 to 6
- depth_kernel: float32 [3, 3, 728], replicated, may hold values from -2 to 2
- point_weight: bfloat16 [728, 728], replicated, may hold values from -0.21875 to 0.21875
- batch_norm_gain: float32 [728], replicated, may hold values from 0.5 to 2
- norm_shift_bias: float32 [728], replicated, may hold values from -1 to 1
Outputs:
- block_out: bfloat16 [32, 4, 16, 728], P(('grp', 'sp'))
- input_grad: bfloat16 [32, 4, 16, 728], P('grp', 'sp')
- weight_grad: float32 [529984], P('sp')
All inputs are finite; a program needn't handle non-finite values.
Results may differ from a plain program's by a relative error of at most 0.018.
Values may be sent and summed in bfloat16 or wider, within the bound.
A program may use at most 64 MiB of HBM per device.

v0:
```python
import jax
import jax.numpy as jnp
from jax import lax
from jax.sharding import PartitionSpec as P


def depth_forward(field, filter_weight):
    rows = field.shape[1]
    cols = field.shape[2]
    padded = jnp.pad(field, ((0, 0), (1, 1), (1, 1), (0, 0)))
    total = jnp.zeros(field.shape, jnp.float32)
    for i in range(3):
        for j in range(3):
            total = total + padded[:, i : i + rows, j : j + cols, :] * filter_weight[i, j]
    return total


def depth_backward(field, filter_weight):
    rows = field.shape[1]
    cols = field.shape[2]
    padded = jnp.pad(field, ((0, 0), (1, 1), (1, 1), (0, 0)))
    total = jnp.zeros(field.shape, jnp.float32)
    for i in range(3):
        for j in range(3):
            total = (
                total
                + padded[:, 2 - i : 2 - i + rows, 2 - j : 2 - j + cols, :] * filter_weight[i, j]
            )
    return total


def body(acts, cotangent, depth_kernel, point_weight, batch_norm_gain, norm_shift_bias):
    channel_count = acts.shape[-1]
    sample_image = lax.all_to_all(acts, "sp", split_axis=0, concat_axis=1, tiled=True)
    input_single_precision = sample_image.astype(jnp.float32)
    hidden = jnp.maximum(input_single_precision, 0.0)
    depthed = depth_forward(hidden, depth_kernel).astype(jnp.bfloat16)
    flat_d = depthed.reshape(-1, channel_count)
    element_count = flat_d.shape[0] * lax.axis_size("sp")
    projected_output = jnp.dot(flat_d, point_weight, preferred_element_type=jnp.float32)
    total, squares = lax.psum(
        (jnp.sum(projected_output, axis=0), jnp.sum(projected_output * projected_output, axis=0)),
        "sp",
    )
    batch_mean = total / element_count
    var = squares / element_count - batch_mean * batch_mean
    inverse_deviation = lax.rsqrt(var + 1e-05)
    normalized_input = (projected_output - batch_mean) * inverse_deviation
    block_out = (
        (
            input_single_precision.reshape(-1, channel_count)
            + batch_norm_gain * normalized_input
            + norm_shift_bias
        )
        .astype(jnp.bfloat16)
        .reshape(sample_image.shape)
    )
    gfloat = cotangent.astype(jnp.float32).reshape(-1, channel_count)
    scaled_output = gfloat * batch_norm_gain
    leading_layer, second_layer = lax.psum(
        (jnp.sum(scaled_output, axis=0), jnp.sum(scaled_output * normalized_input, axis=0)), "sp"
    )
    projected_gradient = (
        inverse_deviation
        * (
            scaled_output
            - leading_layer / element_count
            - normalized_input * (second_layer / element_count)
        )
    ).astype(jnp.bfloat16)
    local_weight = jnp.dot(
        flat_d.T, projected_gradient, preferred_element_type=jnp.float32
    ).reshape(-1)
    ddepth = jnp.dot(
        projected_gradient, point_weight.T, preferred_element_type=jnp.float32
    ).reshape(sample_image.shape)
    dhidden = depth_backward(ddepth, depth_kernel)
    dinput = (
        gfloat.reshape(sample_image.shape) + jnp.where(sample_image > 0, dhidden, 0.0)
    ).astype(jnp.bfloat16)
    input_grad = lax.all_to_all(dinput, "sp", split_axis=1, concat_axis=0, tiled=True)
    slices = lax.psum_scatter(
        local_weight.astype(jnp.bfloat16), "sp", scatter_dimension=0, tiled=True
    ).astype(jnp.float32)
    weight_grad = lax.psum(slices, "grp")
    return (block_out, input_grad, weight_grad)


def solution(mesh):
    in_specs = (P("grp", "sp", None, None), P(("grp", "sp"), None, None, None), P(), P(), P(), P())
    out_specs = (P(("grp", "sp"), None, None, None), P("grp", "sp", None, None), P("sp"))
    return jax.shard_map(body, mesh=mesh, in_specs=in_specs, out_specs=out_specs, check_vma=False)
```

profile of v0, /device:TPU:0, one launch (start us, length us, event | category | flops | bytes accessed | tf_op | source)
XLA Modules:
  0.0 160.6 jit_solution(10437990497592473162)
XLA Ops:
  7.2 0.0 copy-start
  7.2 5.3 %all-to-all-start = ((bf16[4,1,16,728]{3,2,1,0:T(8,128)(2,1)}), bf16[4,1,16,728]{3,2,1,0:T(8,128)(2,1)S(1)}, u32[]{:S(2)}, u32[]{:S(2)}) async-start(bf16[4,1,16,728]{3,2,1,0:T(8,128)(2,1)} %param.6), calls=%async_computation | async-start | bytes 196608 | tf_op jit(solution)/shard_map/all_to_all | solution.py:34
  12.5 0.0 all-reduce.10.cloned.1.call-start
  12.6 1.0 multiply_reduce_fusion.1
  13.5 1.0 slice_reduce_fusion.8
  14.5 3.0 %all-to-all-done = bf16[4,1,16,728]{3,2,1,0:T(8,128)(2,1)S(1)} async-done(((bf16[4,1,16,728]{3,2,1,0:T(8,128)(2,1)}), bf16[4,1,16,728]{3,2,1,0:T(8,128)(2,1)S(1)}, u32[]{:S(2)}, u32[]{:S(2)}) %all-to-all-start) | async-done | bytes 93216 | tf_op jit(solution)/shard_map/all_to_all | solution.py:34
  17.5 0.1 fusion.9
  17.6 0.0 copy-start.3
  17.6 0.0 copy-done
  17.6 0.3 fusion.39
  18.0 8.4 %all-reduce.4 = (f32[728]{0:T(1024)S(1)}, f32[728]{0:T(1024)S(1)}) all-reduce(f32[728]{0:T(1024)S(1)} %get-tuple-element.7, f32[728]{0:T(1024)S(1)} %get-tuple-element.6), channel_id=1, replica_groups=mesh['grp'=8,'sp'=4] {'sp'}, use_global_device_ids=true, to_apply=%region_3.4 | all-reduce | flops 1456 | bytes 11648 | tf_op jit(solution)/shard_map/psum | solution.py:41
  26.5 0.0 copy-done.1
  26.5 0.0 copy-done.2
  26.5 0.1 multiply_reduce_fusion
  26.5 9.0 %all-reduce.3 = (f32[728]{0:T(1024)S(1)}, f32[728]{0:T(1024)S(1)}) all-reduce(f32[728]{0:T(1024)S(1)} %multiply_reduce_fusion, f32[728]{0:T(1024)S(1)} %multiply_reduce_fusion.1), channel_id=1, replica_groups=mesh['grp'=8,'sp'=4] {'sp'}, use_global_device_ids=true, to_apply=%region_7.8 | all-reduce | flops 1456 | bytes 11648 | tf_op jit(solution)/shard_map/psum | solution.py:60
  35.6 0.0 copy-done.3
  35.6 0.7 multiply_convert_fusion
  36.3 0.5 convolution_convert_fusion
  36.8 0.0 copy-start.4
  36.8 3.5 %convert_element_type.59 = bf16[529984]{0:T(1024)(128)(2,1)} reshape(bf16[728,728]{1,0:T(8,128)(2,1)S(1)} %convolution_convert_fusion) | data formatting | bytes 2119936 | tf_op jit(solution)/shard_map/convert_element_type | solution.py:83
  40.3 0.0 all-reduce.10.cloned.1.call-update
  40.3 0.0 all-reduce.8.cloned.1.call-start
  40.3 0.6 dynamic-slice
  41.6 0.5 fusion.40
  42.1 51.5 %all-reduce.10.cloned.1.call-done = bf16[529984]{0:T(1024)(128)(2,1)} async-done(((bf16[529984]{0:T(1024)(128)(2,1)}), bf16[529984]{0:T(1024)(128)(2,1)}) %all-reduce.10.cloned.1.call-update) | async-done | bytes 1059984
  93.5 1.9 %dynamic-slice_convert_fusion = f32[132496]{0:T(1024)} fusion(bf16[529984]{0:T(1024)(128)(2,1)} %all-reduce.10.cloned.1.call-done, u32[]{:T(128)S(6)} %multiply.5), kind=kLoop, calls=%fused_computation.17 | loop fusion | flops 132496 | bytes 794980 | tf_op jit(solution)/shard_map/convert_element_type | solution.py:84
  95.5 0.0 all-reduce.8.cloned.1.call-update
  95.5 0.2 fusion.38
  95.7 7.7 %all_to_all.21 = bf16[1,4,16,728]{3,2,0,1:T(8,128)(2,1)S(1)} all-to-all(bf16[1,4,16,728]{3,2,0,1:T(8,128)(2,1)S(1)} %fusion.38), channel_id=1, replica_groups=mesh['grp'=8,'sp'=4] {'sp'}, dimensions={1} | all-to-all | bytes 186368 | tf_op jit(solution)/shard_map/all_to_all | solution.py:81
  103.4 47.9 %all-reduce.8.cloned.1.call-done = f32[132496]{0:T(1024)} async-done(((f32[132496]{0:T(1024)}), f32[132496]{0:T(1024)}) %all-reduce.8.cloned.1.call-update) | async-done | bytes 530000 | tf_op jit(solution)/shard_map/psum | solution.py:85
  151.3 0.6 copy.16
  151.9 1.9 %copy.17 = f32[132496]{0:T(1024)} copy(f32[132496]{0:T(1024)} %all-reduce.8.cloned.1.call-done) | data formatting | bytes 1059968
  (7 shorter events, 0.1 us)
Async XLA Ops:
  7.2 10.5 %copy-start = (bf16[728,728]{1,0:T(8,128)(2,1)S(1)}, bf16[728,728]{1,0:T(8,128)(2,1)}, u32[]{:S(2)}) copy-start(bf16[728,728]{1,0:T(8,128)(2,1)} %param.9) | copy-start | bytes 3179908
  7.2 10.3 %all-to-all-start = ((bf16[4,1,16,728]{3,2,1,0:T(8,128)(2,1)}), bf16[4,1,16,728]{3,2,1,0:T(8,128)(2,1)S(1)}, u32[]{:S(2)}, u32[]{:S(2)}) async-start(bf16[4,1,16,728]{3,2,1,0:T(8,128)(2,1)} %param.6), calls=%async_computation | async-start | bytes 196608 | tf_op jit(solution)/shard_map/all_to_all | solution.py:34
  12.5 13.9 %copy-start.1 = (bf16[1,4,16,728]{3,2,1,0:T(8,128)(2,1)S(1)}, bf16[1,4,16,728]{3,2,1,0:T(8,128)(2,1)}, u32[]{:S(2)}) copy-start(bf16[1,4,16,728]{3,2,1,0:T(8,128)(2,1)} %param.7) | copy-start | bytes 279556
  12.5 13.9 %copy-start.2 = (f32[728]{0:T(1024)S(1)}, f32[728]{0:T(1024)}, u32[]{:S(2)}) copy-start(f32[728]{0:T(1024)} %param.10) | copy-start | bytes 8740
  12.5 81.0 %all-reduce.10.cloned.1.call-start = ((), (), s32[]{:S(2)}) async-start(), calls=%async_computation.3 | async-start | bytes 2121728
  17.6 18.0 %copy-start.3 = (f32[728]{0:T(1024)S(1)}, f32[728]{0:T(1024)}, u32[]{:S(2)}) copy-start(f32[728]{0:T(1024)} %param.11) | copy-start | bytes 8740
  36.8 3.5 %copy-start.4 = (u32[32]{0:T(128)S(1)}, u32[32]{0:T(128)}, u32[]{:S(2)}) copy-start(u32[32]{0:T(128)} %constant.23) | copy-start | bytes 388
  40.3 111.0 %all-reduce.8.cloned.1.call-start = ((), (), s32[]{:S(2)}) async-start(), calls=%async_computation.2 | async-start | bytes 1064960 | tf_op jit(solution)/shard_map/psum | solution.py:85
Sparse Core Ops, SparseCore 0:
  40.4 53.0 all-reduce.9
  96.5 54.7 all-reduce.7
where the time goes:
time: 161 us
  waiting for transfers between devices  102 us (63%)
  blocking collectives  25.1 us (16%)
  between operations  14.8 us (9%)
  local copies, waits for them, and re-layouts  7.53 us (5%)
  starting transfers between devices  5.41 us (3%)
  other arithmetic  4.04 us (3%)
    unnamed x3, waiting for transfers between devices  51.5 us
    psum x1, waiting for transfers between devices, body(): weight_grad = lax.psum(slices, 'grp')  47.9 us
    psum x1, blocking collectives, body(): lax.psum((jnp.sum(scaled_output, axis=0), jnp.sum(scaled_output * normali...  8.99 us
    psum x1, blocking collectives, body(): lax.psum((jnp.sum(projected_output, axis=0), jnp.sum(projected_output * p...  8.45 us
    all_to_all x1, blocking collectives, body(): lax.all_to_all(dinput, 'sp', split_axis=1, concat_axis=0, tiled=True)  7.68 us
    all_to_all x1, starting transfers between devices, body(): lax.all_to_all(acts, 'sp', split_axis=0, concat_axis=1, tiled=True)  5.34 us
    convert_element_type x1, local copies, waits for them, and re-layouts, body(): local_weight.astype(jnp.bfloat16)  3.46 us
  transfers between devices with their start and end apart: 3, of which 3 were waited for; matrix products, arithmetic and copies ran while one was open for 2% of the time, Pallas kernels for 0%

commit v1 on v0

--- a/solution.py
+++ b/solution.py
@@ -82,7 +82,13 @@
     slices = lax.psum_scatter(
         local_weight.astype(jnp.bfloat16), "sp", scatter_dimension=0, tiled=True
     ).astype(jnp.float32)
-    weight_grad = lax.psum(slices, "grp")
+    peers = lax.axis_size("grp")
+    weight_grad, hop = (slices, 1)
+    while hop < peers:
+        weight_grad = weight_grad + lax.ppermute(
+            weight_grad, "grp", [(i_2, i_2 ^ hop) for i_2 in range(peers)]
+        )
+        hop = 2 * hop
     return (block_out, input_grad, weight_grad)
 
 

time: 161 us -> 147 us (0.913)
  waiting for transfers between devices: 102 us -> 84.4 us
  starting transfers between devices: 5.41 us -> 9.46 us
  local copies, waits for them, and re-layouts: 7.53 us -> 5.66 us
    psum x1 -> x0, waiting for transfers between devices: 47.9 us -> none  [body(): weight_grad = lax.psum(slices, 'grp')]
    ppermute x0 -> x3, waiting for transfers between devices: none -> 29.4 us  [body(): lax.ppermute(weight_grad, 'grp', [(i_2, i_2 ^ hop) for i_2 in range(peers)])]
    ppermute x0 -> x3, starting transfers between devices: none -> 4.09 us  [body(): lax.ppermute(weight_grad, 'grp', [(i_2, i_2 ^ hop) for i_2 in range(peers)])]
    add x0 -> x3, other arithmetic: none -> 2.07 us  [body(): weight_grad + lax.ppermute(weight_grad, 'grp', [(i_2, i_2 ^ hop) for i_2...]
    unnamed x13 -> x12, local copies, waits for them, and re-layouts: 3.13 us -> 1.25 us
    unnamed x3 -> x2, waiting for transfers between devices: 51.5 us -> 52 us
  transfers between devices with their start and end apart: 3 -> 5, of which waited for: 3 -> 5; matrix products, arithmetic and copies ran while one was open for 2% -> 2% of each run, Pallas kernels for 0% -> 0%
where the time goes in v1:
time: 147 us; the launch traced here: 146 us
  waiting for transfers between devices  84.4 us (57%)
  blocking collectives  25.1 us (17%)
  between operations  14.8 us (10%)
  starting transfers between devices  9.46 us (6%)
  local copies, waits for them, and re-layouts  5.66 us (4%)
  other arithmetic  5.31 us (4%)
    unnamed x2, waiting for transfers between devices  52 us
    ppermute x3, waiting for transfers between devices, body(): lax.ppermute(weight_grad, 'grp', [(i_2, i_2 ^ hop) for i_2 in range(peers)])  29.4 us
    psum x1, blocking collectives, body(): lax.psum((jnp.sum(scaled_output, axis=0), jnp.sum(scaled_output * normali...  8.99 us
    psum x1, blocking collectives, body(): lax.psum((jnp.sum(projected_output, axis=0), jnp.sum(projected_output * p...  8.45 us
    all_to_all x1, blocking collectives, body(): lax.all_to_all(dinput, 'sp', split_axis=1, concat_axis=0, tiled=True)  7.68 us
    all_to_all x1, starting transfers between devices, body(): lax.all_to_all(acts, 'sp', split_axis=0, concat_axis=1, tiled=True)  5.34 us
    ppermute x3, starting transfers between devices, body(): lax.ppermute(weight_grad, 'grp', [(i_2, i_2 ^ hop) for i_2 in range(peers)])  4.09 us
    convert_element_type x1, local copies, waits for them, and re-layouts, body(): local_weight.astype(jnp.bfloat16)  3.46 us
  transfers between devices with their start and end apart: 5, of which 5 were waited for; matrix products, arithmetic and copies ran while one was open for 2% of the time, Pallas kernels for 0%

profile of v1, /device:TPU:0, one launch (start us, length us, event | category | flops | bytes accessed | tf_op | source)
XLA Modules:
  0.0 146.1 jit_solution(13561468147204999503)
XLA Ops:
  7.2 0.0 copy-start
  7.2 5.3 %all-to-all-start = ((bf16[4,1,16,728]{3,2,1,0:T(8,128)(2,1)}), bf16[4,1,16,728]{3,2,1,0:T(8,128)(2,1)S(1)}, u32[]{:S(2)}, u32[]{:S(2)}) async-start(bf16[4,1,16,728]{3,2,1,0:T(8,128)(2,1)} %param.6), calls=%async_computation | async-start | bytes 196608 | tf_op jit(solution)/shard_map/all_to_all | solution.py:34
  12.5 0.0 all-reduce.7.cloned.1.call-start
  12.6 1.0 multiply_reduce_fusion.1
  13.5 1.0 slice_reduce_fusion.8
  14.5 3.0 %all-to-all-done = bf16[4,1,16,728]{3,2,1,0:T(8,128)(2,1)S(1)} async-done(((bf16[4,1,16,728]{3,2,1,0:T(8,128)(2,1)}), bf16[4,1,16,728]{3,2,1,0:T(8,128)(2,1)S(1)}, u32[]{:S(2)}, u32[]{:S(2)}) %all-to-all-start) | async-done | bytes 93216 | tf_op jit(solution)/shard_map/all_to_all | solution.py:34
  17.5 0.1 fusion.9
  17.6 0.3 fusion.40
  18.0 8.4 %all-reduce.4 = (f32[728]{0:T(1024)S(1)}, f32[728]{0:T(1024)S(1)}) all-reduce(f32[728]{0:T(1024)S(1)} %get-tuple-element.7, f32[728]{0:T(1024)S(1)} %get-tuple-element.6), channel_id=1, replica_groups=mesh['grp'=8,'sp'=4] {'sp'}, use_global_device_ids=true, to_apply=%region_3.4 | all-reduce | flops 1456 | bytes 11648 | tf_op jit(solution)/shard_map/psum | solution.py:41
  26.5 0.1 multiply_reduce_fusion
  26.5 9.0 %all-reduce.3 = (f32[728]{0:T(1024)S(1)}, f32[728]{0:T(1024)S(1)}) all-reduce(f32[728]{0:T(1024)S(1)} %multiply_reduce_fusion, f32[728]{0:T(1024)S(1)} %multiply_reduce_fusion.1), channel_id=1, replica_groups=mesh['grp'=8,'sp'=4] {'sp'}, use_global_device_ids=true, to_apply=%region_7.8 | all-reduce | flops 1456 | bytes 11648 | tf_op jit(solution)/shard_map/psum | solution.py:60
  35.6 0.7 multiply_convert_fusion
  36.3 0.5 convolution_convert_fusion
  36.8 0.0 copy-start.4
  36.8 3.5 %convert_element_type.59 = bf16[529984]{0:T(1024)(128)(2,1)} reshape(bf16[728,728]{1,0:T(8,128)(2,1)S(1)} %convolution_convert_fusion) | data formatting | bytes 2119936 | tf_op jit(solution)/shard_map/convert_element_type | solution.py:83
  40.3 0.0 all-reduce.7.cloned.1.call-update
  40.3 0.6 dynamic-slice
  41.5 52.0 %all-reduce.7.cloned.1.call-done = bf16[529984]{0:T(1024)(128)(2,1)} async-done(((bf16[529984]{0:T(1024)(128)(2,1)}), bf16[529984]{0:T(1024)(128)(2,1)}) %all-reduce.7.cloned.1.call-update) | async-done | bytes 1059984
  93.5 1.1 dynamic-slice_convert_fusion
  94.7 0.1 collective-permute-start
  94.8 1.9 %collective-permute-done = f32[132496]{0:T(1024)S(1)} collective-permute-done((f32[132496]{0:T(1024)S(1)}, f32[132496]{0:T(1024)S(1)}, u32[]{:S(2)}, u32[]{:S(2)}) %collective-permute-start) | collective-permute-done | bytes 530016 | tf_op jit(solution)/shard_map/ppermute | solution.py:88
  96.7 1.1 fusion.38
  97.8 1.6 %collective-permute-start.1 = (f32[132496]{0:T(1024)S(1)}, f32[132496]{0:T(1024)S(1)}, u32[]{:S(2)}, u32[]{:S(2)}) collective-permute-start(f32[132496]{0:T(1024)S(1)} %fusion.38), channel_id=1, source_target_pairs={{0,8},{4,12},{8,0},{12,4},{16,24},{20,28},{24,16},{28,20},{1,9},{5... | collective-permute-start | bytes 1589960 | tf_op jit(solution)/shard_map/ppermute | solution.py:88
  99.3 12.7 %collective-permute-done.1 = f32[132496]{0:T(1024)S(1)} collective-permute-done((f32[132496]{0:T(1024)S(1)}, f32[132496]{0:T(1024)S(1)}, u32[]{:S(2)}, u32[]{:S(2)}) %collective-permute-start.1) | collective-permute-done | bytes 530016 | tf_op jit(solution)/shard_map/ppermute | solution.py:88
  112.0 0.1 add.114
  112.1 2.5 %collective-permute-start.2 = (f32[132496]{0:T(1024)S(1)}, f32[132496]{0:T(1024)S(1)}, u32[]{:S(2)}, u32[]{:S(2)}) collective-permute-start(f32[132496]{0:T(1024)S(1)} %add.114), channel_id=1, source_target_pairs={{0,16},{4,20},{8,24},{12,28},{16,0},{20,4},{24,8},{28,12},{1,17},{... | collective-permute-start | bytes 1589960 | tf_op jit(solution)/shard_map/ppermute | solution.py:88
  114.5 0.5 fusion.41
  115.0 0.2 fusion.39
  115.2 7.7 %all_to_all.21 = bf16[1,4,16,728]{3,2,0,1:T(8,128)(2,1)S(1)} all-to-all(bf16[1,4,16,728]{3,2,0,1:T(8,128)(2,1)S(1)} %fusion.39), channel_id=1, replica_groups=mesh['grp'=8,'sp'=4] {'sp'}, dimensions={1} | all-to-all | bytes 186368 | tf_op jit(solution)/shard_map/all_to_all | solution.py:81
  122.9 14.9 %collective-permute-done.2 = f32[132496]{0:T(1024)S(1)} collective-permute-done((f32[132496]{0:T(1024)S(1)}, f32[132496]{0:T(1024)S(1)}, u32[]{:S(2)}, u32[]{:S(2)}) %collective-permute-start.2) | collective-permute-done | bytes 530016 | tf_op jit(solution)/shard_map/ppermute | solution.py:88
  137.7 0.9 add.115
  138.6 0.6 copy.15
  (12 shorter events, 0.1 us)
Async XLA Ops:
  7.2 10.5 %copy-start = (bf16[728,728]{1,0:T(8,128)(2,1)S(1)}, bf16[728,728]{1,0:T(8,128)(2,1)}, u32[]{:S(2)}) copy-start(bf16[728,728]{1,0:T(8,128)(2,1)} %param.9) | copy-start | bytes 3179908
  7.2 10.3 %all-to-all-start = ((bf16[4,1,16,728]{3,2,1,0:T(8,128)(2,1)}), bf16[4,1,16,728]{3,2,1,0:T(8,128)(2,1)S(1)}, u32[]{:S(2)}, u32[]{:S(2)}) async-start(bf16[4,1,16,728]{3,2,1,0:T(8,128)(2,1)} %param.6), calls=%async_computation | async-start | bytes 196608 | tf_op jit(solution)/shard_map/all_to_all | solution.py:34
  12.5 13.9 %copy-start.1 = (bf16[1,4,16,728]{3,2,1,0:T(8,128)(2,1)S(1)}, bf16[1,4,16,728]{3,2,1,0:T(8,128)(2,1)}, u32[]{:S(2)}) copy-start(bf16[1,4,16,728]{3,2,1,0:T(8,128)(2,1)} %param.7) | copy-start | bytes 279556
  12.5 13.9 %copy-start.2 = (f32[728]{0:T(1024)S(1)}, f32[728]{0:T(1024)}, u32[]{:S(2)}) copy-start(f32[728]{0:T(1024)} %param.10) | copy-start | bytes 8740
  12.5 81.0 %all-reduce.7.cloned.1.call-start = ((), (), s32[]{:S(2)}) async-start(), calls=%async_computation.2 | async-start | bytes 2121728
  17.6 18.0 %copy-start.3 = (f32[728]{0:T(1024)S(1)}, f32[728]{0:T(1024)}, u32[]{:S(2)}) copy-start(f32[728]{0:T(1024)} %param.11) | copy-start | bytes 8740
  36.8 3.5 %copy-start.4 = (u32[32]{0:T(128)S(1)}, u32[32]{0:T(128)}, u32[]{:S(2)}) copy-start(u32[32]{0:T(128)} %constant.23) | copy-start | bytes 388
  94.7 2.0 %collective-permute-start = (f32[132496]{0:T(1024)S(1)}, f32[132496]{0:T(1024)S(1)}, u32[]{:S(2)}, u32[]{:S(2)}) collective-permute-start(f32[132496]{0:T(1024)S(1)} %dynamic-slice_convert_fusion), channel_id=1, source_target_pairs={{0,4},{4,0},{8,12},{12,8},{16,20},{20,16},{24,28},{28,24},{1,5},{5... | collective-permute-start | bytes 1589960 | tf_op jit(solution)/shard_map/ppermute | solution.py:88
  97.8 14.2 %collective-permute-start.1 = (f32[132496]{0:T(1024)S(1)}, f32[132496]{0:T(1024)S(1)}, u32[]{:S(2)}, u32[]{:S(2)}) collective-permute-start(f32[132496]{0:T(1024)S(1)} %fusion.38), channel_id=1, source_target_pairs={{0,8},{4,12},{8,0},{12,4},{16,24},{20,28},{24,16},{28,20},{1,9},{5... | collective-permute-start | bytes 1589960 | tf_op jit(solution)/shard_map/ppermute | solution.py:88
  112.1 25.7 %collective-permute-start.2 = (f32[132496]{0:T(1024)S(1)}, f32[132496]{0:T(1024)S(1)}, u32[]{:S(2)}, u32[]{:S(2)}) collective-permute-start(f32[132496]{0:T(1024)S(1)} %add.114), channel_id=1, source_target_pairs={{0,16},{4,20},{8,24},{12,28},{16,0},{20,4},{24,8},{28,12},{1,17},{... | collective-permute-start | bytes 1589960 | tf_op jit(solution)/shard_map/ppermute | solution.py:88
Sparse Core Ops, SparseCore 0:
  40.4 53.0 all-reduce.6
